TPU v7x, 32 devices: a whole 2x2x4 slice. The times are simulated.
32 devices in a mesh: ch: 4 (over z), ha: 2 (over x), dp: 4 (over y, core).
Axes of the slice: x: 2, y: 2, z: 4, core: 2. Of those that a mesh axis runs over, the one named last changes fastest.
Arguments:
- features: bfloat16 [384, 4, 4, 4, 128], P('ch', 'dp', None, 'ha'), may hold values from -26 to 26
- frame_count: int32 [4], P('dp'), may hold values from 1 to 4, as said below
- norm1_gain: float32 [384], P('ch'), may hold values from 0.5 to 2
- norm1_shift: float32 [384], P('ch'), may hold values from -3 to 3
- qkv_weight: bfloat16 [384, 1152], replicated, may hold values from -0.51031036 to 0.51031036
- qkv_bias: float32 [1152], replicated, may hold values from -3 to 3
- out_weight: bfloat16 [384, 384], replicated, may hold values from -0.3125 to 0.3125
- out_bias: float32 [384], replicated, may hold values from -3 to 3
- norm2_gain: float32 [384], P('ch'), may hold values from 0.5 to 2
- norm2_shift: float32 [384], P('ch'), may hold values from -3 to 3
- conv_weight: bfloat16 [3, 3, 3, 384, 384], P(None, None, None, 'ch'), may hold values from -0.0625 to 0.0625
- conv_bias: float32 [384], P('ch'), may hold values from -3 to 3
- cotangent: bfloat16 [384, 4, 4, 4, 128], P('ch', 'dp', None, 'ha'), may hold values from -0.0625 to 0.0625
Outputs:
- mixed: bfloat16 [384, 4, 4, 4, 128], P('ch', 'dp', None, 'ha')
- weight_grad: float32 [3, 3, 3, 384, 384], P(None, None, None, 'ch')
Inputs may be any that keep to these rules, and one draw needn't show every extreme that they name: `frame_count`: some clip has all 4 frames valid and some clip only one.
All inputs are finite; a program needn't handle non-finite values.
Results may differ from a plain program's by a relative error of at most 0.015.
Values may be sent and summed in bfloat16 or wider, within the bound.
A program may use at most 64 MiB of HBM per device.

v0:
```python
import jax
import jax.numpy as jnp
from jax import lax
from jax.sharding import PartitionSpec as P

GROUPS = 32
EPS = 1e-06


def padded_2(x, sides, width):
    for axis, dim in sides:
        count, length = (lax.axis_size(axis), x.shape[dim])
        up = [(i, (i + 1) % count) for i in range(count - 1)]
        down = [(j, i) for i, j in up]
        last = lax.slice_in_dim(x, length - width, length, axis=dim)
        leading = lax.slice_in_dim(x, 0, width, axis=dim)
        before = lax.ppermute(last, axis, up)
        after = lax.ppermute(leading, axis, down)
        x = jnp.concatenate([before, x, after], axis=dim)
    return x


def frame_mask(frame_count, frames):
    position = lax.broadcasted_iota(jnp.int32, (frame_count.shape[0], frames), 1)
    return (position < frame_count[:, None]).astype(jnp.float32)


def moments(values, mask, groups):
    chans, clips, frames, rows, cols = values.shape
    data = values.astype(jnp.float32).reshape(groups, chans // groups, clips, frames, rows * cols)
    first = jnp.einsum("gkbfp,bf->gb", data, mask)
    second = jnp.einsum("gkbfp,bf->gb", data * data, mask)
    return (first, second)


def normalize(values, first, second, count, gain, shift, groups):
    chans, clips, frames, rows, cols = values.shape
    mean = first / count[None, :]
    var = second / count[None, :] - mean * mean
    scale = lax.rsqrt(var + EPS)
    data = values.astype(jnp.float32).reshape(groups, chans // groups, clips, frames, rows * cols)
    normed = (data - mean[:, None, :, None, None]) * scale[:, None, :, None, None]
    normed = normed.reshape(values.shape)
    return normed * gain[:, None, None, None, None] + shift[:, None, None, None, None]


def attend(carry, queries, keys, values, scale):
    top, total, acc = carry
    scores = jnp.einsum("itc,isc->its", queries, keys, preferred_element_type=jnp.float32) * scale
    new_top = jnp.max(scores, axis=2)
    factor = jnp.exp(top - new_top)
    weights = jnp.exp(scores - new_top[..., None])
    total = total * factor + jnp.sum(weights, axis=2)
    acc = acc * factor[..., None] + jnp.einsum(
        "its,isc->itc", weights.astype(jnp.bfloat16), values, preferred_element_type=jnp.float32
    )
    return (new_top, total, acc)


def tap_stack(padded, time_tap, frames, rows, cols):
    windows = []
    for row_tap in range(3):
        for col_tap in range(3):
            windows.append(
                padded[
                    :,
                    :,
                    time_tap : time_tap + frames,
                    row_tap : row_tap + rows,
                    col_tap : col_tap + cols,
                ]
            )
    return jnp.concatenate(windows, axis=0)


def butterfly_sum(table, axes):
    steps = []
    for axis in axes:
        size = lax.axis_size(axis)
        for bit in range(size.bit_length() - 1):
            steps.append((axis, bit, size))
    length = table.shape[0]
    unit = (1 << len(steps)) * 8
    padded = -(-length // unit) * unit
    work = jnp.pad(table, ((0, padded - length), (0, 0)))
    for axis, bit, size in steps:
        side = lax.axis_index(axis) >> bit & 1
        halves = work.reshape(2, work.shape[0] // 2, work.shape[1])
        keep = lax.dynamic_index_in_dim(halves, side, keepdims=False)
        send = lax.dynamic_index_in_dim(halves, 1 - side, keepdims=False)
        perm = [(i, i ^ 1 << bit) for i in range(size)]
        got = lax.ppermute(send.astype(jnp.bfloat16), axis, perm)
        work = keep + got.astype(jnp.float32)
    work = work.astype(jnp.bfloat16)
    for axis, bit, size in reversed(steps):
        side = lax.axis_index(axis) >> bit & 1
        perm = [(i, i ^ 1 << bit) for i in range(size)]
        got = lax.ppermute(work, axis, perm)
        pair = jnp.stack([work, got])
        first = lax.dynamic_index_in_dim(pair, side, keepdims=False)
        second = lax.dynamic_index_in_dim(pair, 1 - side, keepdims=False)
        work = jnp.concatenate([first, second], axis=0)
    return work[:length].astype(jnp.float32)


def doubling_sum(values, axis):
    size = lax.axis_size(axis)
    for bit in range(size.bit_length() - 1):
        perm = [(i, i ^ 1 << bit) for i in range(size)]
        got = lax.ppermute(values, axis, perm)
        values = tuple((a + b for a, b in zip(values, got)))
    return values


def body(
    features,
    frame_count,
    norm1_gain,
    norm1_shift,
    qkv_weight,
    qkv_bias,
    out_weight,
    out_bias,
    norm2_gain,
    norm2_shift,
    conv_weight,
    conv_bias,
    cotangent,
):
    chans, clips, frames, rows, cols = features.shape
    groups = GROUPS // lax.axis_size("ch")
    mask = frame_mask(frame_count, frames)
    count = frame_count.astype(jnp.float32) * (chans // groups * rows * lax.axis_size("ha") * cols)
    first, second = moments(features, mask, groups)
    first, second = doubling_sum((first, second), "ha")
    normed = normalize(features, first, second, count, norm1_gain, norm1_shift, groups).astype(
        jnp.bfloat16
    )
    by_frame = lax.all_to_all(normed, "ch", split_axis=2, concat_axis=0, tiled=True)
    width = by_frame.shape[0]
    items = clips * by_frame.shape[2]
    tok_rows = rows * cols
    tokens = by_frame.reshape(width, items, tok_rows)
    queries = lax.dot_general(
        tokens, qkv_weight[:, :width], (((0,), (0,)), ((), ())), preferred_element_type=jnp.float32
    )
    queries = (queries + qkv_bias[:width]).astype(jnp.bfloat16)
    scale = width ** (-0.5)
    start_carry = (
        jnp.full((items, tok_rows), -jnp.inf, jnp.float32),
        jnp.zeros((items, tok_rows), jnp.float32),
        jnp.zeros((items, tok_rows, width), jnp.float32),
    )
    pairs = lax.dot_general(
        tokens, qkv_weight[:, width:], (((0,), (0,)), ((), ())), preferred_element_type=jnp.float32
    )
    pairs = (pairs + qkv_bias[width:]).astype(jnp.bfloat16)
    piece = lax.all_gather(pairs, "ha", axis=1, tiled=True)
    top, total, acc = attend(start_carry, queries, piece[..., :width], piece[..., width:], scale)
    attended = (acc / total[..., None]).astype(jnp.bfloat16)
    projected = lax.dot_general(
        out_weight, attended, (((0,), (2,)), ((), ())), preferred_element_type=jnp.float32
    )
    projected = (projected + out_bias[:, None, None]).astype(jnp.bfloat16).reshape(by_frame.shape)
    update = lax.all_to_all(projected, "ch", split_axis=0, concat_axis=2, tiled=True)
    hidden = (features.astype(jnp.float32) + update.astype(jnp.float32)).astype(jnp.bfloat16)
    first, second = moments(hidden, mask, groups)
    first, second = doubling_sum((first, second), "ha")
    gated = jax.nn.silu(
        normalize(hidden, first, second, count, norm2_gain, norm2_shift, groups)
    ).astype(jnp.bfloat16)
    with_rows = padded_2(gated, (("ha", 3),), 1)
    padded = jnp.pad(with_rows, ((0, 0), (0, 0), (2, 0), (0, 0), (1, 1)))
    stacks = [tap_stack(padded, time_tap, frames, rows, cols) for time_tap in range(3)]
    amount = chans * lax.axis_size("ch")
    summed = jnp.zeros((amount, clips, frames, rows, cols), jnp.float32)
    for time_tap in range(3):
        part = conv_weight[time_tap].reshape(9 * chans, amount)
        summed = summed + lax.dot_general(
            part, stacks[time_tap], (((0,), (0,)), ((), ())), preferred_element_type=jnp.float32
        )
    summed, stacks = lax.optimization_barrier((summed.astype(jnp.bfloat16), stacks))
    shares = lax.axis_size("ch")
    parts = summed.reshape((shares, amount // shares) + summed.shape[1:])
    parts = lax.all_to_all(parts, "ch", split_axis=0, concat_axis=0, tiled=True)
    conv_out = jnp.sum(parts.astype(jnp.float32), axis=0)
    mixed = mask[None, :, :, None, None] * (
        hidden.astype(jnp.float32) + conv_out + conv_bias[:, None, None, None, None]
    )
    mixed = mixed.astype(jnp.bfloat16)
    masked_cot = cotangent * mask.astype(jnp.bfloat16)[None, :, :, None, None]
    full_width = chans * lax.axis_size("ch")
    carry = jnp.zeros((3, 9 * chans, full_width), jnp.float32)
    copies = jnp.broadcast_to(masked_cot[None], (shares,) + masked_cot.shape)
    piece = lax.all_to_all(copies, "ch", split_axis=0, concat_axis=0, tiled=True)
    piece = piece.reshape((shares * chans,) + masked_cot.shape[1:])
    start = jnp.int32(0)
    for time_tap in range(3):
        part = lax.dot_general(
            stacks[time_tap],
            piece,
            (((1, 2, 3, 4), (1, 2, 3, 4)), ((), ())),
            preferred_element_type=jnp.float32,
        )
        carry = lax.dynamic_update_slice(
            carry, part[None], (jnp.int32(time_tap), jnp.int32(0), start)
        )
    weight_grad = butterfly_sum(carry.reshape(27 * chans, full_width), ("dp", "ha"))
    weight_grad = weight_grad.reshape(3, 3, 3, chans, full_width)
    return (mixed, weight_grad)


def solution(mesh):
    placed = (
        P("ch", "dp", None, "ha", None),
        P("dp"),
        P("ch"),
        P("ch"),
        P(),
        P(),
        P(),
        P(),
        P("ch"),
        P("ch"),
        P(None, None, None, "ch", None),
        P("ch"),
        P("ch", "dp", None, "ha", None),
    )
    return jax.shard_map(
        body,
        mesh=mesh,
        in_specs=placed,
        out_specs=(P("ch", "dp", None, "ha", None), P(None, None, None, "ch", None)),
        check_vma=False,
    )
```

profile of v0, /device:TPU:0, one launch (start us, length us, event | category | flops | bytes accessed | tf_op | source)
XLA Modules:
  0.0 152.2 jit_solution(14878665267219705704)
XLA Ops:
  1.3 1.1 fusion.65
  2.8 3.0 %collective-permute-start = (f32[8,1]{0,1:T(1,128)S(1)}, f32[8,1]{0,1:T(1,128)S(1)}, u32[]{:S(2)}, u32[]{:S(2)}) collective-permute-start(f32[8,1]{0,1:T(1,128)S(1)} %convolution_bitcast_fusion.3), channel_id=1, source_target_pairs={{0,4},{4,0},{1,5},{5,1},{2,6},{6,2},{3,7},{7,3},{8,12},{12,8},{9,1... | collective-permute-start | bytes 104 | tf_op jit(solution)/shard_map/ppermute | solution.py:110
  6.1 1.2 collective-permute-done
  7.3 2.3 %collective-permute-done.1 = f32[8,1]{0,1:T(1,128)S(1)} collective-permute-done((f32[8,1]{0,1:T(1,128)S(1)}, f32[8,1]{0,1:T(1,128)S(1)}, u32[]{:S(2)}, u32[]{:S(2)}) %collective-permute-start.1) | collective-permute-done | bytes 64 | tf_op jit(solution)/shard_map/ppermute | solution.py:110
  9.9 1.8 %fusion.91 = bf16[96,1,4,2,128]{4,0,3,1,2:T(8,128)(2,1)} fusion(f32[96]{0:T(128)} %param.16, f32[96]{0:T(128)} %param.15, f32[96]{0:T(128)S(1)} %mul.117, f32[96]{0:T(128)S(1)} %sub.78, bf16[96,1,4,2,128]{4,3,2,1,0:T(2,128)(2,1)} %param.13), kind=kLoop, calls=%fused_computation.119 | loop fusion | flops 589824 | bytes 394752 | tf_op jit(solution)/shard_map/convert_element_type | solution.py:136
  11.8 5.0 %all-to-all-start = ((bf16[96,1,4,2,128]{4,0,3,1,2:T(8,128)(2,1)}), bf16[96,1,4,2,128]{4,0,3,1,2:T(8,128)(2,1)S(1)}, u32[]{:S(2)}, u32[]{:S(2)}) async-start(bf16[96,1,4,2,128]{4,0,3,1,2:T(8,128)(2,1)} %fusion.91), calls=%async_computation | async-start | bytes 393216 | tf_op jit(solution)/shard_map/all_to_all | solution.py:139
  17.5 5.5 %all-to-all-done = bf16[96,1,4,2,128]{4,0,3,1,2:T(8,128)(2,1)S(1)} async-done(((bf16[96,1,4,2,128]{4,0,3,1,2:T(8,128)(2,1)}), bf16[96,1,4,2,128]{4,0,3,1,2:T(8,128)(2,1)S(1)}, u32[]{:S(2)}, u32[]{:S(2)}) %all-to-all-start) | async-done | bytes 196640 | tf_op jit(solution)/shard_map/all_to_all | solution.py:139
  23.2 1.5 fusion.37
  24.6 8.7 %all-gather = bf16[512,768]{1,0:T(8,128)(2,1)S(1)} all-gather(bf16[256,768]{1,0:T(8,128)(2,1)S(1)} %fusion.37), channel_id=2, replica_groups=mesh['ch'=4,'ha'=2,'dp'=4] {'ha'}, dimensions={0}, use_global_device_ids=true | all-gather | bytes 1179648 | tf_op jit(solution)/shard_map/all_gather | solution.py:158
  33.3 1.6 %fusion.119 = (f32[256]{0:T(256)S(1)}, f32[256,512]{1,0:T(8,128)S(1)}) fusion(bf16[1,512,768]{2,1,0:T(8,128)(2,1)S(1)} %bitcast.223, bf16[384,1152]{1,0:T(8,128)(2,1)} %param.17, f32[384]{0:T(512)S(1)} %slice-done, bf16[48,8,2,128]{3,2,1,0:T(2,128)(2,1)S(1)} %bitcast.232), kind=kOutput, calls=%fused_computation.180 | convolution fusion | flops 176619264 | bytes 1412096 | tf_op jit(solution)/shard_map/itc,isc->its/dot_general | solution.py:49
  35.7 0.9 copy.28
  36.6 3.4 %all-to-all-start.1 = ((bf16[384,1,1,2,128]{4,3,2,1,0:T(2,128)(2,1)}), bf16[384,1,1,2,128]{4,3,2,1,0:T(2,128)(2,1)S(1)}, u32[]{:S(2)}, u32[]{:S(2)}) async-start(bf16[384,1,1,2,128]{4,3,2,1,0:T(2,128)(2,1)} %copy.28), calls=%async_computation.1 | async-start | bytes 393216 | tf_op jit(solution)/shard_map/all_to_all | solution.py:165
  40.3 5.9 %all-to-all-done.1 = bf16[384,1,1,2,128]{4,3,2,1,0:T(2,128)(2,1)S(1)} async-done(((bf16[384,1,1,2,128]{4,3,2,1,0:T(2,128)(2,1)}), bf16[384,1,1,2,128]{4,3,2,1,0:T(2,128)(2,1)S(1)}, u32[]{:S(2)}, u32[]{:S(2)}) %all-to-all-start.1) | async-done | bytes 196640 | tf_op jit(solution)/shard_map/all_to_all | solution.py:165
  46.2 1.0 broadcast_in_dim.17
  47.2 3.5 %all-to-all-start.3 = ((bf16[4,96,1,4,2,128]{5,1,4,3,2,0:T(8,128)(2,1)}), bf16[4,96,1,4,2,128]{5,1,4,3,2,0:T(8,128)(2,1)S(1)}, u32[]{:S(2)}, u32[]{:S(2)}) async-start(bf16[4,96,1,4,2,128]{5,1,4,3,2,0:T(8,128)(2,1)} %broadcast_in_dim.17), calls=%async_computation.3 | async-start | bytes 1572864 | tf_op jit(solution)/shard_map/all_to_all | solution.py:195
  52.1 1.5 collective-permute-start.3
  53.6 1.2 collective-permute-done.2
  56.4 3.4 %collective-permute-start.4 = (bf16[96,1,4,1,128]{4,0,3,2,1:T(8,128)(2,1)S(1)}, bf16[96,1,4,1,128]{4,0,3,2,1:T(8,128)(2,1)S(1)}, u32[]{:S(2)}, u32[]{:S(2)}) collective-permute-start(bf16[96,1,4,1,128]{4,0,3,2,1:T(8,128)(2,1)S(1)} %get-tuple-element.61), channel_id=1, source_target_pairs={{0,4},{1,5},{2,6},{3,7},{8,12},{9,13},{10,14},{11,15},{16,20},{17,... | collective-permute-start | bytes 294920 | tf_op jit(solution)/shard_map/ppermute | solution.py:17
  59.8 1.5 collective-permute-start.5
  61.3 2.6 %fusion.117 = (bf16[1,3,3,96,384]{4,3,2,1,0:T(8,128)(2,1)}, bf16[1,3,3,96,384]{4,3,2,1,0:T(8,128)(2,1)S(1)}, bf16[1,3,3,96,384]{4,3,2,1,0:T(8,128)(2,1)S(1)}) fusion(bf16[3,3,3,96,384]{4,3,2,1,0:T(8,128)(2,1)} %param.23), kind=kLoop, calls=%fused_computation.178 | loop fusion | bytes 3981312 | tf_op jit(solution)/shard_map/slice | solution.py:178
  63.9 2.5 %collective-permute-done.5 = bf16[96,1,4,1,128]{4,0,3,2,1:T(8,128)(2,1)S(1)} collective-permute-done((bf16[96,1,4,1,128]{4,0,3,2,1:T(8,128)(2,1)S(1)}, bf16[96,1,4,1,128]{4,0,3,2,1:T(8,128)(2,1)S(1)}, u32[]{:S(2)}, u32[]{:S(2)}) %collective-permute-start.5) | collective-permute-done | bytes 98336 | tf_op jit(solution)/shard_map/ppermute | solution.py:18
  69.3 1.2 fusion.13
  70.5 1.2 fusion.15
  71.8 1.3 fusion.34
  73.1 2.6 %fusion.19 = f32[1,864,384]{2,1,0:T(8,128)S(1)} fusion(bf16[384,4,2,128]{3,0,2,1:T(8,128)(2,1)S(1)} %bitcast.225, bf16[864,1,4,2,128]{4,0,3,2,1:T(8,128)(2,1)} %copy-done.7), kind=kOutput, calls=%fused_computation.29 | convolution fusion | flops 679477248 | bytes 3883008 | tf_op jit(solution)/shard_map/dot_general | solution.py:199
  76.0 1.2 copy-done.6
  77.2 1.1 fusion.25
  78.7 1.1 fusion.31
  80.1 1.9 %copy-done.1 = f32[2624,384]{1,0:T(8,128)} copy-done((f32[2624,384]{1,0:T(8,128)}, f32[2624,384]{1,0:T(8,128)S(1)}, u32[]{:S(2)}) %copy-start.1) | copy-done | bytes 4030488
  82.2 2.7 %collective-permute-done.6 = bf16[1312,384]{1,0:T(8,128)(2,1)} collective-permute-done((bf16[1312,384]{1,0:T(8,128)(2,1)S(1)}, bf16[1312,384]{1,0:T(8,128)(2,1)}, u32[]{:S(2)}, u32[]{:S(2)}) %collective-permute-start.6) | collective-permute-done | bytes 1007648 | tf_op jit(solution)/shard_map/ppermute | solution.py:92
  84.9 2.0 %bitcast_add_fusion = f32[1312,384]{1,0:T(8,128)S(1)} fusion(bf16[1312,384]{1,0:T(8,128)(2,1)} %collective-permute-done.6, f32[2,1312,384]{2,1,0:T(8,128)} %bitcast.214, s32[]{:T(128)S(6)} %select_n.30), kind=kLoop, calls=%fused_computation.12 | loop fusion | flops 1007616 | bytes 5038084 | tf_op jit(solution)/shard_map/add | solution.py:93
  87.8 1.5 %collective-permute-start.7 = (bf16[656,384]{1,0:T(8,128)(2,1)}, bf16[656,384]{1,0:T(8,128)(2,1)}, u32[]{:S(2)}, u32[]{:S(2)}) collective-permute-start(bf16[656,384]{1,0:T(8,128)(2,1)} %fusion.53), channel_id=1, source_target_pairs={{0,2},{1,3},{2,0},{3,1},{4,6},{5,7},{6,4},{7,5},{8,10},{9,11},{10,... | collective-permute-start | bytes 1511432 | tf_op jit(solution)/shard_map/ppermute | solution.py:92
  89.3 12.3 %collective-permute-done.7 = bf16[656,384]{1,0:T(8,128)(2,1)} collective-permute-done((bf16[656,384]{1,0:T(8,128)(2,1)}, bf16[656,384]{1,0:T(8,128)(2,1)}, u32[]{:S(2)}, u32[]{:S(2)}) %collective-permute-start.7) | collective-permute-done | bytes 503840 | tf_op jit(solution)/shard_map/ppermute | solution.py:92
  101.6 2.1 %bitcast_add_fusion.1 = f32[656,384]{1,0:T(8,128)} fusion(bf16[656,384]{1,0:T(8,128)(2,1)} %collective-permute-done.7, f32[2,656,384]{2,1,0:T(8,128)S(1)} %bitcast.217, s32[]{:T(128)S(6)} %select_n.32), kind=kLoop, calls=%fused_computation.64 | loop fusion | flops 503808 | bytes 2519044 | tf_op jit(solution)/shard_map/add | solution.py:93
  103.7 1.1 fusion.86
  105.0 7.1 %collective-permute-done.8 = bf16[328,384]{1,0:T(8,128)(2,1)S(1)} collective-permute-done((bf16[328,384]{1,0:T(8,128)(2,1)S(1)}, bf16[328,384]{1,0:T(8,128)(2,1)S(1)}, u32[]{:S(2)}, u32[]{:S(2)}) %collective-permute-start.8) | collective-permute-done | bytes 251936 | tf_op jit(solution)/shard_map/ppermute | solution.py:92
  112.1 1.1 fusion.58
  113.5 6.1 %collective-permute-done.9 = bf16[328,384]{1,0:T(8,128)(2,1)S(1)} collective-permute-done((bf16[328,384]{1,0:T(8,128)(2,1)S(1)}, bf16[328,384]{1,0:T(8,128)(2,1)S(1)}, u32[]{:S(2)}, u32[]{:S(2)}) %collective-permute-start.9) | collective-permute-done | bytes 251936 | tf_op jit(solution)/shard_map/ppermute | solution.py:98
  119.9 1.1 pad_maximum_fusion.2
  120.9 1.5 %collective-permute-start.10 = (bf16[656,384]{1,0:T(8,128)(2,1)}, bf16[656,384]{1,0:T(8,128)(2,1)}, u32[]{:S(2)}, u32[]{:S(2)}) collective-permute-start(bf16[656,384]{1,0:T(8,128)(2,1)} %get-tuple-element.57), channel_id=1, source_target_pairs={{0,2},{1,3},{2,0},{3,1},{4,6},{5,7},{6,4},{7,5},{8,10},{9,11},{10,... | collective-permute-start | bytes 1511432 | tf_op jit(solution)/shard_map/ppermute | solution.py:98
  122.9 1.0 copy.32
  123.9 5.1 %all-to-all-start.2 = ((bf16[4,96,1,4,2,128]{5,1,4,3,2,0:T(8,128)(2,1)}), bf16[4,96,1,4,2,128]{5,1,4,3,2,0:T(8,128)(2,1)S(1)}, u32[]{:S(2)}, u32[]{:S(2)}) async-start(bf16[4,96,1,4,2,128]{5,1,4,3,2,0:T(8,128)(2,1)} %copy.32), calls=%async_computation.2 | async-start | bytes 1572864 | tf_op jit(solution)/shard_map/all_to_all | solution.py:185
  128.9 3.3 %collective-permute-done.10 = bf16[656,384]{1,0:T(8,128)(2,1)} collective-permute-done((bf16[656,384]{1,0:T(8,128)(2,1)}, bf16[656,384]{1,0:T(8,128)(2,1)}, u32[]{:S(2)}, u32[]{:S(2)}) %collective-permute-start.10) | collective-permute-done | bytes 503840 | tf_op jit(solution)/shard_map/ppermute | solution.py:98
  132.2 1.5 fusion.57
  133.7 1.1 pad_maximum_fusion.1
  134.8 11.7 %all-to-all-done.2 = bf16[4,96,1,4,2,128]{5,1,4,3,2,0:T(8,128)(2,1)S(1)} async-done(((bf16[4,96,1,4,2,128]{5,1,4,3,2,0:T(8,128)(2,1)}), bf16[4,96,1,4,2,128]{5,1,4,3,2,0:T(8,128)(2,1)S(1)}, u32[]{:S(2)}, u32[]{:S(2)}) %all-to-all-start.2) | async-done | bytes 786464 | tf_op jit(solution)/shard_map/all_to_all | solution.py:185
  147.6 2.0 %fusion.51 = (bf16[1312,384]{1,0:T(8,128)(2,1)S(1)}, bf16[1312,384]{1,0:T(8,128)(2,1)S(1)}) fusion(s32[]{:T(128)S(6)} %select_n.30, bf16[1,1312,384]{2,1,0:T(8,128)(2,1)S(1)} %get-tuple-element.54, bf16[1,1312,384]{2,1,0:T(8,128)(2,1)} %bitcast.78, s32[]{:T(128)S(6)} %select_n.31), kind=kLoop, calls=%fused_computation.62 | loop fusion | flops 1007616 | bytes 4030472 | tf_op jit(solution)/shard_map/jit(dynamic_index_in_dim)/squeeze | solution.py:100
  149.8 2.4 %convert.5 = f32[3,3,3,96,384]{4,3,2,1,0:T(8,128)} convert(bf16[3,3,3,96,384]{4,3,2,1,0:T(8,128)(2,1)S(1)} %bitcast.215) | non-fusion elementwise | flops 995328 | bytes 5971968 | tf_op jit(solution)/shard_map/reshape | solution.py:209
  (100 shorter events, 13.1 us)
Async XLA Ops:
  0.6 34.5 %copy-start = (bf16[384,384]{1,0:T(8,128)(2,1)S(1)}, bf16[384,384]{1,0:T(8,128)(2,1)}, u32[]{:S(2)}) copy-start(bf16[384,384]{1,0:T(8,128)(2,1)} %param.19) | copy-start | bytes 884740
  2.8 4.5 %collective-permute-start = (f32[8,1]{0,1:T(1,128)S(1)}, f32[8,1]{0,1:T(1,128)S(1)}, u32[]{:S(2)}, u32[]{:S(2)}) collective-permute-start(f32[8,1]{0,1:T(1,128)S(1)} %convolution_bitcast_fusion.3), channel_id=1, source_target_pairs={{0,4},{4,0},{1,5},{5,1},{2,6},{6,2},{3,7},{7,3},{8,12},{12,8},{9,1... | collective-permute-start | bytes 104 | tf_op jit(solution)/shard_map/ppermute | solution.py:110
  6.0 3.6 %collective-permute-start.1 = (f32[8,1]{0,1:T(1,128)S(1)}, f32[8,1]{0,1:T(1,128)S(1)}, u32[]{:S(2)}, u32[]{:S(2)}) collective-permute-start(f32[8,1]{0,1:T(1,128)S(1)} %convolution_bitcast_fusion.2), channel_id=1, source_target_pairs={{0,4},{4,0},{1,5},{5,1},{2,6},{6,2},{3,7},{7,3},{8,12},{12,8},{9,1... | collective-permute-start | bytes 104 | tf_op jit(solution)/shard_map/ppermute | solution.py:110
  11.8 21.5 %slice-start = ((f32[1152]{0:T(1024)}), f32[384]{0:T(512)S(1)}, s32[]{:S(2)}) async-start(f32[1152]{0:T(1024)} %param.18), calls=%async_computation.4 | async-start | bytes 4096 | tf_op jit(solution)/shard_map/slice | solution.py:147
  11.8 11.3 %all-to-all-start = ((bf16[96,1,4,2,128]{4,0,3,1,2:T(8,128)(2,1)}), bf16[96,1,4,2,128]{4,0,3,1,2:T(8,128)(2,1)S(1)}, u32[]{:S(2)}, u32[]{:S(2)}) async-start(bf16[96,1,4,2,128]{4,0,3,1,2:T(8,128)(2,1)} %fusion.91), calls=%async_computation | async-start | bytes 393216 | tf_op jit(solution)/shard_map/all_to_all | solution.py:139
  24.6 10.5 %copy-start.14 = (f32[384]{0:T(512)S(1)}, f32[384]{0:T(512)}, u32[]{:S(2)}) copy-start(f32[384]{0:T(512)} %param.20) | copy-start | bytes 4612
  35.2 4.8 %copy-start.10 = (bf16[96,1,4,2,128]{4,3,2,1,0:T(2,128)(2,1)S(1)}, bf16[96,1,4,2,128]{4,3,2,1,0:T(2,128)(2,1)}, u32[]{:S(2)}) copy-start(bf16[96,1,4,2,128]{4,3,2,1,0:T(2,128)(2,1)} %param.25) | copy-start | bytes 589828
  36.6 9.6 %all-to-all-start.1 = ((bf16[384,1,1,2,128]{4,3,2,1,0:T(2,128)(2,1)}), bf16[384,1,1,2,128]{4,3,2,1,0:T(2,128)(2,1)S(1)}, u32[]{:S(2)}, u32[]{:S(2)}) async-start(bf16[384,1,1,2,128]{4,3,2,1,0:T(2,128)(2,1)} %copy.28), calls=%async_computation.1 | async-start | bytes 393216 | tf_op jit(solution)/shard_map/all_to_all | solution.py:165
  40.2 10.5 %copy-start.9 = (bf16[96,1,4,2,128]{4,3,2,1,0:T(2,128)(2,1)S(1)}, bf16[96,1,4,2,128]{4,3,2,1,0:T(2,128)(2,1)}, u32[]{:S(2)}) copy-start(bf16[96,1,4,2,128]{4,3,2,1,0:T(2,128)(2,1)} %param.13) | copy-start | bytes 589828
  40.3 15.8 %copy-start.11 = (f32[96]{0:T(128)S(1)}, f32[96]{0:T(128)}, u32[]{:S(2)}) copy-start(f32[96]{0:T(128)} %param.22) | copy-start | bytes 1156
  40.3 15.7 %copy-start.12 = (f32[96]{0:T(128)S(1)}, f32[96]{0:T(128)}, u32[]{:S(2)}) copy-start(f32[96]{0:T(128)} %param.21) | copy-start | bytes 1156
  47.2 25.8 %all-to-all-start.3 = ((bf16[4,96,1,4,2,128]{5,1,4,3,2,0:T(8,128)(2,1)}), bf16[4,96,1,4,2,128]{5,1,4,3,2,0:T(8,128)(2,1)S(1)}, u32[]{:S(2)}, u32[]{:S(2)}) async-start(bf16[4,96,1,4,2,128]{5,1,4,3,2,0:T(8,128)(2,1)} %broadcast_in_dim.17), calls=%async_computation.3 | async-start | bytes 1572864 | tf_op jit(solution)/shard_map/all_to_all | solution.py:195
  51.3 3.6 %collective-permute-start.2 = (f32[8,1]{0,1:T(1,128)S(1)}, f32[8,1]{0,1:T(1,128)S(1)}, u32[]{:S(2)}, u32[]{:S(2)}) collective-permute-start(f32[8,1]{0,1:T(1,128)S(1)} %convolution_bitcast_fusion.1), channel_id=1, source_target_pairs={{0,4},{4,0},{1,5},{5,1},{2,6},{6,2},{3,7},{7,3},{8,12},{12,8},{9,1... | collective-permute-start | bytes 104 | tf_op jit(solution)/shard_map/ppermute | solution.py:110
  52.1 3.6 %collective-permute-start.3 = (f32[8,1]{0,1:T(1,128)S(1)}, f32[8,1]{0,1:T(1,128)S(1)}, u32[]{:S(2)}, u32[]{:S(2)}) collective-permute-start(f32[8,1]{0,1:T(1,128)S(1)} %convolution_bitcast_fusion), channel_id=1, source_target_pairs={{0,4},{4,0},{1,5},{5,1},{2,6},{6,2},{3,7},{7,3},{8,12},{12,8},{9,1... | collective-permute-start | bytes 104 | tf_op jit(solution)/shard_map/ppermute | solution.py:110
  56.4 7.5 %collective-permute-start.4 = (bf16[96,1,4,1,128]{4,0,3,2,1:T(8,128)(2,1)S(1)}, bf16[96,1,4,1,128]{4,0,3,2,1:T(8,128)(2,1)S(1)}, u32[]{:S(2)}, u32[]{:S(2)}) collective-permute-start(bf16[96,1,4,1,128]{4,0,3,2,1:T(8,128)(2,1)S(1)} %get-tuple-element.61), channel_id=1, source_target_pairs={{0,4},{1,5},{2,6},{3,7},{8,12},{9,13},{10,14},{11,15},{16,20},{17,... | collective-permute-start | bytes 294920 | tf_op jit(solution)/shard_map/ppermute | solution.py:17
  59.8 6.5 %collective-permute-start.5 = (bf16[96,1,4,1,128]{4,0,3,2,1:T(8,128)(2,1)S(1)}, bf16[96,1,4,1,128]{4,0,3,2,1:T(8,128)(2,1)S(1)}, u32[]{:S(2)}, u32[]{:S(2)}) collective-permute-start(bf16[96,1,4,1,128]{4,0,3,2,1:T(8,128)(2,1)S(1)} %get-tuple-element.62), channel_id=1, source_target_pairs={{4,0},{5,1},{6,2},{7,3},{12,8},{13,9},{14,10},{15,11},{20,16},{21,... | collective-permute-start | bytes 294920 | tf_op jit(solution)/shard_map/ppermute | solution.py:18
  68.1 1.2 copy-start.2
  69.1 1.5 copy-start.5
  69.1 2.7 %copy-start.7 = (bf16[864,1,4,2,128]{4,0,3,2,1:T(8,128)(2,1)}, bf16[864,1,4,2,128]{4,0,3,2,1:T(8,128)(2,1)S(1)}, u32[]{:S(2)}) copy-start(bf16[864,1,4,2,128]{4,0,3,2,1:T(8,128)(2,1)S(1)} %get-tuple-element.7) | copy-start | bytes 5308420
  69.3 2.5 %copy-start.3 = (bf16[864,1,4,2,128]{4,0,3,2,1:T(8,128)(2,1)}, bf16[864,1,4,2,128]{4,0,3,2,1:T(8,128)(2,1)S(1)}, u32[]{:S(2)}) copy-start(bf16[864,1,4,2,128]{4,0,3,2,1:T(8,128)(2,1)S(1)} %slice_dynamic-update-slice_fusion) | copy-start | bytes 5308420
  75.7 1.5 copy-start.6
  77.2 1.5 copy-start.4
  80.0 1.9 %copy-start.1 = (f32[2624,384]{1,0:T(8,128)}, f32[2624,384]{1,0:T(8,128)S(1)}, u32[]{:S(2)}) copy-start(f32[2624,384]{1,0:T(8,128)S(1)} %pad.10) | copy-start | bytes 12091396
  82.1 2.8 %collective-permute-start.6 = (bf16[1312,384]{1,0:T(8,128)(2,1)S(1)}, bf16[1312,384]{1,0:T(8,128)(2,1)}, u32[]{:S(2)}, u32[]{:S(2)}) collective-permute-start(bf16[1312,384]{1,0:T(8,128)(2,1)S(1)} %fusion.47), channel_id=1, source_target_pairs={{0,1},{1,0},{2,3},{3,2},{4,5},{5,4},{6,7},{7,6},{8,9},{9,8},{10,11... | collective-permute-start | bytes 3022856 | tf_op jit(solution)/shard_map/ppermute | solution.py:92
  87.8 13.8 %collective-permute-start.7 = (bf16[656,384]{1,0:T(8,128)(2,1)}, bf16[656,384]{1,0:T(8,128)(2,1)}, u32[]{:S(2)}, u32[]{:S(2)}) collective-permute-start(bf16[656,384]{1,0:T(8,128)(2,1)} %fusion.53), channel_id=1, source_target_pairs={{0,2},{1,3},{2,0},{3,1},{4,6},{5,7},{6,4},{7,5},{8,10},{9,11},{10,... | collective-permute-start | bytes 1511432 | tf_op jit(solution)/shard_map/ppermute | solution.py:92
  104.8 7.3 %collective-permute-start.8 = (bf16[328,384]{1,0:T(8,128)(2,1)S(1)}, bf16[328,384]{1,0:T(8,128)(2,1)S(1)}, u32[]{:S(2)}, u32[]{:S(2)}) collective-permute-start(bf16[328,384]{1,0:T(8,128)(2,1)S(1)} %fusion.86), channel_id=1, source_target_pairs={{0,4},{4,0},{1,5},{5,1},{2,6},{6,2},{3,7},{7,3},{8,12},{12,8},{9,1... | collective-permute-start | bytes 755720 | tf_op jit(solution)/shard_map/ppermute | solution.py:92
  113.2 6.5 %collective-permute-start.9 = (bf16[328,384]{1,0:T(8,128)(2,1)S(1)}, bf16[328,384]{1,0:T(8,128)(2,1)S(1)}, u32[]{:S(2)}, u32[]{:S(2)}) collective-permute-start(bf16[328,384]{1,0:T(8,128)(2,1)S(1)} %fusion.58), channel_id=1, source_target_pairs={{0,4},{4,0},{1,5},{5,1},{2,6},{6,2},{3,7},{7,3},{8,12},{12,8},{9,1... | collective-permute-start | bytes 755720 | tf_op jit(solution)/shard_map/ppermute | solution.py:98
  120.9 11.3 %collective-permute-start.10 = (bf16[656,384]{1,0:T(8,128)(2,1)}, bf16[656,384]{1,0:T(8,128)(2,1)}, u32[]{:S(2)}, u32[]{:S(2)}) collective-permute-start(bf16[656,384]{1,0:T(8,128)(2,1)} %get-tuple-element.57), channel_id=1, source_target_pairs={{0,2},{1,3},{2,0},{3,1},{4,6},{5,7},{6,4},{7,5},{8,10},{9,11},{10,... | collective-permute-start | bytes 1511432 | tf_op jit(solution)/shard_map/ppermute | solution.py:98
  122.9 9.3 %copy-start.8 = (bf16[1,656,384]{2,1,0:T(8,128)(2,1)S(1)}, bf16[1,656,384]{2,1,0:T(8,128)(2,1)}, u32[]{:S(2)}) copy-start(bf16[1,656,384]{2,1,0:T(8,128)(2,1)} %get-tuple-element.58) | copy-start | bytes 1511428
  123.9 22.6 %all-to-all-start.2 = ((bf16[4,96,1,4,2,128]{5,1,4,3,2,0:T(8,128)(2,1)}), bf16[4,96,1,4,2,128]{5,1,4,3,2,0:T(8,128)(2,1)S(1)}, u32[]{:S(2)}, u32[]{:S(2)}) async-start(bf16[4,96,1,4,2,128]{5,1,4,3,2,0:T(8,128)(2,1)} %copy.32), calls=%async_computation.2 | async-start | bytes 1572864 | tf_op jit(solution)/shard_map/all_to_all | solution.py:185
  133.7 12.9 %copy-start.13 = (f32[96]{0:T(128)S(1)}, f32[96]{0:T(128)}, u32[]{:S(2)}) copy-start(f32[96]{0:T(128)} %param.24) | copy-start | bytes 1156
  134.8 12.8 %collective-permute-start.11 = (bf16[1312,384]{1,0:T(8,128)(2,1)}, bf16[1312,384]{1,0:T(8,128)(2,1)}, u32[]{:S(2)}, u32[]{:S(2)}) collective-permute-start(bf16[1312,384]{1,0:T(8,128)(2,1)} %get-tuple-element.53), channel_id=1, source_target_pairs={{0,1},{1,0},{2,3},{3,2},{4,5},{5,4},{6,7},{7,6},{8,9},{9,8},{10,11... | collective-permute-start | bytes 3022856 | tf_op jit(solution)/shard_map/ppermute | solution.py:98
where the time goes:
time: 153 us; the launch traced here: 152 us
  waiting for transfers between devices  62.7 us (41%)
  starting transfers between devices  30.6 us (20%)
  other arithmetic  19.2 us (13%)
  local copies, waits for them, and re-layouts  16.6 us (11%)
  matrix products  12.6 us (8%)
  blocking collectives  8.66 us (6%)
  between operations  1.87 us (1%)
    ppermute x3, waiting for transfers between devices, butterfly_sum(): got = lax.ppermute(send.astype(jnp.bfloat16), axis, perm)  22.1 us
    all_to_all x1, waiting for transfers between devices, body(): parts = lax.all_to_all(parts, 'ch', split_axis=0, concat_axis=0, tiled=True)  11.7 us
    ppermute x3, waiting for transfers between devices, butterfly_sum(): got = lax.ppermute(work, axis, perm)  9.43 us
    all_gather x1, blocking collectives, body(): piece = lax.all_gather(pairs, 'ha', axis=1, tiled=True)  8.66 us
    unnamed x39, local copies, waits for them, and re-layouts  5.97 us
    all_to_all x1, waiting for transfers between devices, body(): lax.all_to_all(projected, 'ch', split_axis=0, concat_axis=2, tiled=True)  5.88 us
    ppermute x4, waiting for transfers between devices, doubling_sum(): got = lax.ppermute(values, axis, perm)  5.65 us
    all_to_all x1, waiting for transfers between devices, body(): lax.all_to_all(normed, 'ch', split_axis=2, concat_axis=0, tiled=True)  5.55 us
  transfers between devices with their start and end apart: 16, of which 13 were waited for; matrix products, arithmetic and copies ran while one was open for 11% of the time, Pallas kernels for 0%

commit v1 on v0

--- a/solution.py
+++ b/solution.py
@@ -5,6 +5,28 @@
 
 GROUPS = 32
 EPS = 1e-06
+
+
+def split_up(x, dim, length):
+    before, after = (x.shape[:dim], x.shape[dim + 1 :])
+    return jnp.moveaxis(x.reshape(*before, length, -1, *after), dim, 0)
+
+
+def joined_along(blocks, dim):
+    blocks = jnp.moveaxis(blocks, 0, dim)
+    shape = blocks.shape
+    return blocks.reshape(*shape[:dim], shape[dim] * shape[dim + 1], *shape[dim + 2 :])
+
+
+def pairwise_exchange(shard, axis, split_dim, concat_dim):
+    length, position = (lax.axis_size(axis), lax.axis_index(axis))
+    pieces = split_up(shard, split_dim, length)
+    done = [pieces[position]]
+    for hop in range(1, length):
+        sent = pieces[position ^ hop]
+        done.append(lax.ppermute(sent, axis, [(i, i ^ hop) for i in range(length)]))
+    pieces = jnp.stack(done)[position ^ jnp.arange(length)]
+    return joined_along(pieces, concat_dim)
 
 
 def padded_2(x, sides, width):
@@ -192,7 +214,7 @@
     full_width = chans * lax.axis_size("ch")
     carry = jnp.zeros((3, 9 * chans, full_width), jnp.float32)
     copies = jnp.broadcast_to(masked_cot[None], (shares,) + masked_cot.shape)
-    piece = lax.all_to_all(copies, "ch", split_axis=0, concat_axis=0, tiled=True)
+    piece = pairwise_exchange(copies, "ch", 0, 0)
     piece = piece.reshape((shares * chans,) + masked_cot.shape[1:])
     start = jnp.int32(0)
     for time_tap in range(3):

time: 153 us -> 149 us (0.974)
  waiting for transfers between devices: 62.7 us -> 51.9 us
  starting transfers between devices: 30.6 us -> 36.4 us
  other arithmetic: 19.2 us -> 22.9 us
  matrix products: 12.6 us -> 9.13 us
    all_to_all x1, waiting for transfers between devices: 5.55 us -> 0.01 us  [body(): lax.all_to_all(normed, 'ch', split_axis=2, concat_axis=0, tiled=True)]
    ppermute x0 -> x3, starting transfers between devices: none -> 4.39 us  [pairwise_exchange(): done.append(lax.ppermute(sent, axis, [(i, i ^ hop) for i in range(length)]))]
    all_to_all x1 -> x0, starting transfers between devices: 3.49 us -> none  [body(): lax.all_to_all(copies, 'ch', split_axis=0, concat_axis=0, tiled=True)]
    ppermute x3, starting transfers between devices: 1.84 us -> 4.91 us  [butterfly_sum(): got = lax.ppermute(send.astype(jnp.bfloat16), axis, perm)]
    gather x0 -> x1, local copies, waits for them, and re-layouts: none -> 2.96 us  [pairwise_exchange(): pieces = jnp.stack(done)[position ^ jnp.arange(length)]]
    another operation x0 -> x1, other arithmetic: none -> 2.68 us  [pairwise_exchange(): pieces = jnp.stack(done)[position ^ jnp.arange(length)]]
    ppermute x1, waiting for transfers between devices: 2.46 us -> 0.01 us  [padded_2(): after = lax.ppermute(leading, axis, down)]
    squeeze x3, other arithmetic: 3.7 us -> 1.45 us  [butterfly_sum(): first = lax.dynamic_index_in_dim(pair, side, keepdims=False)]
  transfers between devices with their start and end apart: 16 -> 18, of which waited for: 13 -> 11; matrix products, arithmetic and copies ran while one was open for 11% -> 13% of each run, Pallas kernels for 0% -> 0%
where the time goes in v1:
time: 149 us; the launch traced here: 148 us
  waiting for transfers between devices  51.9 us (35%)
  starting transfers between devices  36.4 us (24%)
  other arithmetic  22.9 us (15%)
  local copies, waits for them, and re-layouts  16.6 us (11%)
  matrix products  9.13 us (6%)
  blocking collectives  8.97 us (6%)
  between operations  1.84 us (1%)
    ppermute x3, waiting for transfers between devices, butterfly_sum(): got = lax.ppermute(send.astype(jnp.bfloat16), axis, perm)  20.6 us
    all_to_all x1, waiting for transfers between devices, body(): parts = lax.all_to_all(parts, 'ch', split_axis=0, concat_axis=0, tiled=True)  11.5 us
    ppermute x3, waiting for transfers between devices, butterfly_sum(): got = lax.ppermute(work, axis, perm)  9.8 us
    all_gather x1, blocking collectives, body(): piece = lax.all_gather(pairs, 'ha', axis=1, tiled=True)  8.97 us
    ppermute x4, waiting for transfers between devices, doubling_sum(): got = lax.ppermute(values, axis, perm)  5.63 us
    unnamed x29, local copies, waits for them, and re-layouts  5.28 us
    ppermute x4, starting transfers between devices, doubling_sum(): got = lax.ppermute(values, axis, perm)  5.03 us
    ppermute x3, starting transfers between devices, butterfly_sum(): got = lax.ppermute(send.astype(jnp.bfloat16), axis, perm)  4.91 us
  transfers between devices with their start and end apart: 18, of which 11 were waited for; matrix products, arithmetic and copies ran while one was open for 13% of the time, Pallas kernels for 0%

profile of v1, /device:TPU:0, one launch (start us, length us, event | category | flops | bytes accessed | tf_op | source)
XLA Modules:
  0.0 147.8 jit_solution(7012015875894893071)
XLA Ops:
  1.4 1.1 fusion.68
  2.8 3.0 %collective-permute-start = (f32[8,1]{0,1:T(1,128)S(1)}, f32[8,1]{0,1:T(1,128)S(1)}, u32[]{:S(2)}, u32[]{:S(2)}) collective-permute-start(f32[8,1]{0,1:T(1,128)S(1)} %convolution_bitcast_fusion.3), channel_id=1, source_target_pairs={{0,4},{4,0},{1,5},{5,1},{2,6},{6,2},{3,7},{7,3},{8,12},{12,8},{9,1... | collective-permute-start | bytes 104 | tf_op jit(solution)/shard_map/ppermute | solution.py:132
  6.1 1.2 collective-permute-done
  7.4 2.3 %collective-permute-done.1 = f32[8,1]{0,1:T(1,128)S(1)} collective-permute-done((f32[8,1]{0,1:T(1,128)S(1)}, f32[8,1]{0,1:T(1,128)S(1)}, u32[]{:S(2)}, u32[]{:S(2)}) %collective-permute-start.1) | collective-permute-done | bytes 64 | tf_op jit(solution)/shard_map/ppermute | solution.py:132
  10.0 1.8 %fusion.94 = bf16[96,1,4,2,128]{4,0,3,1,2:T(8,128)(2,1)} fusion(f32[96]{0:T(128)} %param.16, f32[96]{0:T(128)} %param.15, f32[96]{0:T(128)S(1)} %mul.117, f32[96]{0:T(128)S(1)} %sub.78, bf16[96,1,4,2,128]{4,3,2,1,0:T(2,128)(2,1)} %param.13), kind=kLoop, calls=%fused_computation.124 | loop fusion | flops 589824 | bytes 394752 | tf_op jit(solution)/shard_map/convert_element_type | solution.py:158
  11.8 4.9 %all-to-all-start = ((bf16[96,1,4,2,128]{4,0,3,1,2:T(8,128)(2,1)}), bf16[96,1,4,2,128]{4,0,3,1,2:T(8,128)(2,1)S(1)}, u32[]{:S(2)}, u32[]{:S(2)}) async-start(bf16[96,1,4,2,128]{4,0,3,1,2:T(8,128)(2,1)} %fusion.94), calls=%async_computation | async-start | bytes 393216 | tf_op jit(solution)/shard_map/all_to_all | solution.py:161
  16.7 2.0 %multiply_bitcast_fusion.1 = (bf16[1,1,96,1,4,2,128]{6,5,4,2,3,1,0:T(2,128)(2,1)}, bf16[1,96,1,4,2,128]{5,4,3,1,2,0:T(2,128)(2,1)}) fusion(bf16[96,1,4,2,128]{4,3,2,1,0:T(2,128)(2,1)} %param.25, bf16[4]{0:T(256)(128)(2,1)S(1)} %fusion.116), kind=kLoop, calls=%fused_computation.161 | loop fusion | flops 98304 | bytes 589832 | tf_op jit(solution)/shard_map/reshape | solution.py:12
  18.6 2.0 %collective-permute-start.6 = (bf16[1,96,1,4,2,128]{5,4,3,1,2,0:T(2,128)(2,1)}, bf16[1,96,1,4,2,128]{5,4,3,1,2,0:T(2,128)(2,1)}, u32[]{:S(2)}, u32[]{:S(2)}) collective-permute-start(bf16[1,96,1,4,2,128]{5,4,3,1,2,0:T(2,128)(2,1)} %get-tuple-element.62), channel_id=1, source_target_pairs={{0,8},{8,0},{16,24},{24,16},{1,9},{9,1},{17,25},{25,17},{2,10},{10... | collective-permute-start | bytes 589832 | tf_op jit(solution)/shard_map/ppermute | solution.py:27
  20.7 2.4 %collective-permute-start.7 = (bf16[1,96,1,4,2,128]{5,4,3,1,2,0:T(2,128)(2,1)}, bf16[1,96,1,4,2,128]{5,4,3,1,2,0:T(2,128)(2,1)}, u32[]{:S(2)}, u32[]{:S(2)}) collective-permute-start(bf16[1,96,1,4,2,128]{5,4,3,1,2,0:T(2,128)(2,1)} %get-tuple-element.62), channel_id=1, source_target_pairs={{0,16},{8,24},{16,0},{24,8},{1,17},{9,25},{17,1},{25,9},{2,18},{10... | collective-permute-start | bytes 589832 | tf_op jit(solution)/shard_map/ppermute | solution.py:27
  24.3 9.0 %all-gather = bf16[512,768]{1,0:T(8,128)(2,1)S(1)} all-gather(bf16[256,768]{1,0:T(8,128)(2,1)S(1)} %fusion.37), channel_id=2, replica_groups=mesh['ch'=4,'ha'=2,'dp'=4] {'ha'}, dimensions={0}, use_global_device_ids=true | all-gather | bytes 1179648 | tf_op jit(solution)/shard_map/all_gather | solution.py:180
  35.6 4.8 %all-to-all-start.1 = ((bf16[384,1,1,2,128]{4,3,2,1,0:T(2,128)(2,1)}), bf16[384,1,1,2,128]{4,3,2,1,0:T(2,128)(2,1)S(1)}, u32[]{:S(2)}, u32[]{:S(2)}) async-start(bf16[384,1,1,2,128]{4,3,2,1,0:T(2,128)(2,1)} %copy.32), calls=%async_computation.1 | async-start | bytes 393216 | tf_op jit(solution)/shard_map/all_to_all | solution.py:187
  40.5 1.8 %fusion.121 = (bf16[1,3,3,96,384]{4,3,2,1,0:T(8,128)(2,1)S(1)}, bf16[1,3,3,96,384]{4,3,2,1,0:T(8,128)(2,1)S(1)}, bf16[1,3,3,96,384]{4,3,2,1,0:T(8,128)(2,1)S(1)}) fusion(bf16[3,3,3,96,384]{4,3,2,1,0:T(8,128)(2,1)} %param.23), kind=kLoop, calls=%fused_computation.187 | loop fusion | bytes 3981312 | tf_op jit(solution)/shard_map/slice | solution.py:200
  42.3 4.4 %all-to-all-done.1 = bf16[384,1,1,2,128]{4,3,2,1,0:T(2,128)(2,1)S(1)} async-done(((bf16[384,1,1,2,128]{4,3,2,1,0:T(2,128)(2,1)}), bf16[384,1,1,2,128]{4,3,2,1,0:T(2,128)(2,1)S(1)}, u32[]{:S(2)}, u32[]{:S(2)}) %all-to-all-start.1) | async-done | bytes 196640 | tf_op jit(solution)/shard_map/all_to_all | solution.py:187
  48.1 1.5 %collective-permute-start.3 = (f32[8,1]{0,1:T(1,128)S(1)}, f32[8,1]{0,1:T(1,128)S(1)}, u32[]{:S(2)}, u32[]{:S(2)}) collective-permute-start(f32[8,1]{0,1:T(1,128)S(1)} %convolution_bitcast_fusion), channel_id=1, source_target_pairs={{0,4},{4,0},{1,5},{5,1},{2,6},{6,2},{3,7},{7,3},{8,12},{12,8},{9,1... | collective-permute-start | bytes 104 | tf_op jit(solution)/shard_map/ppermute | solution.py:132
  49.6 1.2 collective-permute-done.2
  53.0 4.0 %collective-permute-start.4 = (bf16[96,1,4,1,128]{4,0,3,2,1:T(8,128)(2,1)}, bf16[96,1,4,1,128]{4,0,3,2,1:T(8,128)(2,1)}, u32[]{:S(2)}, u32[]{:S(2)}) collective-permute-start(bf16[96,1,4,1,128]{4,0,3,2,1:T(8,128)(2,1)} %get-tuple-element.63), channel_id=1, source_target_pairs={{0,4},{1,5},{2,6},{3,7},{8,12},{9,13},{10,14},{11,15},{16,20},{17,... | collective-permute-start | bytes 294920 | tf_op jit(solution)/shard_map/ppermute | solution.py:39
  57.1 1.3 collective-permute-start.5
  58.4 2.7 %maximum_bitcast_fusion = bf16[4,96,4,2,128]{4,3,2,1,0:T(2,128)(2,1)S(1)} fusion(bf16[1,1,96,1,4,2,128]{6,5,4,2,3,1,0:T(2,128)(2,1)} %bitcast.50, bf16[1,1,96,1,4,2,128]{6,5,4,2,3,1,0:T(2,128)(2,1)} %bitcast.49, bf16[1,1,96,1,4,2,128]{6,5,4,2,3,1,0:T(2,128)(2,1)} %bitcast.48, bf16[1,1,96,1,4,2,128]{6,5,4,2,3,1,0:T(2,128)(2,1)} %get-tuple-element.61), kind=kLoop, calls=%fused_computation.67 | loop fusion | flops 1179648 | bytes 1572864 | tf_op jit(solution)/shard_map/stack | solution.py:28
  61.1 3.0 %gather_fusion = bf16[4,96,4,2,128]{4,3,2,1,0:T(2,128)(2,1)} fusion(bf16[4,96,4,2,128]{4,3,2,1,0:T(2,128)(2,1)S(1)} %maximum_bitcast_fusion, s32[1024]{0:T(1024)S(1)} %pad_clamp_fusion), kind=kCustom, calls=%fused_computation | custom fusion | bytes 1572880 | tf_op jit(solution)/shard_map/gather | solution.py:28
  64.0 1.3 fusion.41
  66.2 0.9 fusion.99
  68.6 0.9 fusion.98
  69.7 1.2 fusion.13
  70.9 1.2 fusion.15
  72.2 1.3 fusion.34
  73.4 1.1 fusion.19
  74.8 1.1 fusion.25
  75.9 1.1 fusion.31
  77.3 1.9 %copy-done.1 = f32[2624,384]{1,0:T(8,128)} copy-done((f32[2624,384]{1,0:T(8,128)}, f32[2624,384]{1,0:T(8,128)S(1)}, u32[]{:S(2)}) %copy-start.1) | copy-done | bytes 4030488
  79.4 2.7 %collective-permute-done.9 = bf16[1312,384]{1,0:T(8,128)(2,1)} collective-permute-done((bf16[1312,384]{1,0:T(8,128)(2,1)S(1)}, bf16[1312,384]{1,0:T(8,128)(2,1)}, u32[]{:S(2)}, u32[]{:S(2)}) %collective-permute-start.9) | collective-permute-done | bytes 1007648 | tf_op jit(solution)/shard_map/ppermute | solution.py:114
  82.1 2.0 %bitcast_add_fusion = f32[1312,384]{1,0:T(8,128)S(1)} fusion(bf16[1312,384]{1,0:T(8,128)(2,1)} %collective-permute-done.9, f32[2,1312,384]{2,1,0:T(8,128)} %bitcast.220, s32[]{:T(128)S(6)} %select_n.45), kind=kLoop, calls=%fused_computation.13 | loop fusion | flops 1007616 | bytes 5038084 | tf_op jit(solution)/shard_map/add | solution.py:115
  85.0 1.5 %collective-permute-start.10 = (bf16[656,384]{1,0:T(8,128)(2,1)}, bf16[656,384]{1,0:T(8,128)(2,1)}, u32[]{:S(2)}, u32[]{:S(2)}) collective-permute-start(bf16[656,384]{1,0:T(8,128)(2,1)} %fusion.56), channel_id=1, source_target_pairs={{0,2},{1,3},{2,0},{3,1},{4,6},{5,7},{6,4},{7,5},{8,10},{9,11},{10,... | collective-permute-start | bytes 1511432 | tf_op jit(solution)/shard_map/ppermute | solution.py:114
  86.5 12.3 %collective-permute-done.10 = bf16[656,384]{1,0:T(8,128)(2,1)} collective-permute-done((bf16[656,384]{1,0:T(8,128)(2,1)}, bf16[656,384]{1,0:T(8,128)(2,1)}, u32[]{:S(2)}, u32[]{:S(2)}) %collective-permute-start.10) | collective-permute-done | bytes 503840 | tf_op jit(solution)/shard_map/ppermute | solution.py:114
  98.8 1.1 bitcast_add_fusion.1
  100.0 0.9 copy-done.2
  100.9 3.3 %collective-permute-start.11 = (bf16[328,384]{1,0:T(8,128)(2,1)S(1)}, bf16[328,384]{1,0:T(8,128)(2,1)S(1)}, u32[]{:S(2)}, u32[]{:S(2)}) collective-permute-start(bf16[328,384]{1,0:T(8,128)(2,1)S(1)} %fusion.89), channel_id=1, source_target_pairs={{0,4},{4,0},{1,5},{5,1},{2,6},{6,2},{3,7},{7,3},{8,12},{12,8},{9,1... | collective-permute-start | bytes 755720 | tf_op jit(solution)/shard_map/ppermute | solution.py:114
  104.3 5.5 %collective-permute-done.11 = bf16[328,384]{1,0:T(8,128)(2,1)S(1)} collective-permute-done((bf16[328,384]{1,0:T(8,128)(2,1)S(1)}, bf16[328,384]{1,0:T(8,128)(2,1)S(1)}, u32[]{:S(2)}, u32[]{:S(2)}) %collective-permute-start.11) | collective-permute-done | bytes 251936 | tf_op jit(solution)/shard_map/ppermute | solution.py:114
  109.8 1.1 fusion.61
  110.9 1.8 %collective-permute-start.12 = (bf16[328,384]{1,0:T(8,128)(2,1)S(1)}, bf16[328,384]{1,0:T(8,128)(2,1)S(1)}, u32[]{:S(2)}, u32[]{:S(2)}) collective-permute-start(bf16[328,384]{1,0:T(8,128)(2,1)S(1)} %fusion.61), channel_id=1, source_target_pairs={{0,4},{4,0},{1,5},{5,1},{2,6},{6,2},{3,7},{7,3},{8,12},{12,8},{9,1... | collective-permute-start | bytes 755720 | tf_op jit(solution)/shard_map/ppermute | solution.py:120
  112.7 5.0 %collective-permute-done.12 = bf16[328,384]{1,0:T(8,128)(2,1)S(1)} collective-permute-done((bf16[328,384]{1,0:T(8,128)(2,1)S(1)}, bf16[328,384]{1,0:T(8,128)(2,1)S(1)}, u32[]{:S(2)}, u32[]{:S(2)}) %collective-permute-start.12) | collective-permute-done | bytes 251936 | tf_op jit(solution)/shard_map/ppermute | solution.py:120
  117.9 0.9 pad_maximum_fusion.2
  118.7 1.5 %collective-permute-start.13 = (bf16[656,384]{1,0:T(8,128)(2,1)}, bf16[656,384]{1,0:T(8,128)(2,1)S(1)}, u32[]{:S(2)}, u32[]{:S(2)}) collective-permute-start(bf16[656,384]{1,0:T(8,128)(2,1)} %get-tuple-element.57), channel_id=1, source_target_pairs={{0,2},{1,3},{2,0},{3,1},{4,6},{5,7},{6,4},{7,5},{8,10},{9,11},{10,... | collective-permute-start | bytes 1511432 | tf_op jit(solution)/shard_map/ppermute | solution.py:120
  120.6 1.0 copy.36
  121.6 3.7 %all-to-all-start.2 = ((bf16[4,96,1,4,2,128]{5,1,4,3,2,0:T(8,128)(2,1)}), bf16[4,96,1,4,2,128]{5,1,4,3,2,0:T(8,128)(2,1)S(1)}, u32[]{:S(2)}, u32[]{:S(2)}) async-start(bf16[4,96,1,4,2,128]{5,1,4,3,2,0:T(8,128)(2,1)} %copy.36), calls=%async_computation.2 | async-start | bytes 1572864 | tf_op jit(solution)/shard_map/all_to_all | solution.py:207
  125.3 4.8 %collective-permute-done.13 = bf16[656,384]{1,0:T(8,128)(2,1)S(1)} collective-permute-done((bf16[656,384]{1,0:T(8,128)(2,1)}, bf16[656,384]{1,0:T(8,128)(2,1)S(1)}, u32[]{:S(2)}, u32[]{:S(2)}) %collective-permute-start.13) | collective-permute-done | bytes 503840 | tf_op jit(solution)/shard_map/ppermute | solution.py:120
  130.6 1.1 pad_maximum_fusion.1
  131.7 11.5 %all-to-all-done.2 = bf16[4,96,1,4,2,128]{5,1,4,3,2,0:T(8,128)(2,1)S(1)} async-done(((bf16[4,96,1,4,2,128]{5,1,4,3,2,0:T(8,128)(2,1)}), bf16[4,96,1,4,2,128]{5,1,4,3,2,0:T(8,128)(2,1)S(1)}, u32[]{:S(2)}, u32[]{:S(2)}) %all-to-all-start.2) | async-done | bytes 786464 | tf_op jit(solution)/shard_map/all_to_all | solution.py:207
  145.3 2.4 %convert.5 = f32[3,3,3,96,384]{4,3,2,1,0:T(8,128)} convert(bf16[3,3,3,96,384]{4,3,2,1,0:T(8,128)(2,1)S(1)} %bitcast.221) | non-fusion elementwise | flops 995328 | bytes 5971968 | tf_op jit(solution)/shard_map/reshape | solution.py:231
  (95 shorter events, 15.1 us)
Async XLA Ops:
  0.6 33.6 %copy-start = (bf16[384,384]{1,0:T(8,128)(2,1)S(1)}, bf16[384,384]{1,0:T(8,128)(2,1)}, u32[]{:S(2)}) copy-start(bf16[384,384]{1,0:T(8,128)(2,1)} %param.19) | copy-start | bytes 884740
  0.6 23.3 %copy-start.8 = (bf16[384,1152]{1,0:T(8,128)(2,1)S(1)}, bf16[384,1152]{1,0:T(8,128)(2,1)}, u32[]{:S(2)}) copy-start(bf16[384,1152]{1,0:T(8,128)(2,1)} %param.17) | copy-start | bytes 2654212
  2.8 4.5 %collective-permute-start = (f32[8,1]{0,1:T(1,128)S(1)}, f32[8,1]{0,1:T(1,128)S(1)}, u32[]{:S(2)}, u32[]{:S(2)}) collective-permute-start(f32[8,1]{0,1:T(1,128)S(1)} %convolution_bitcast_fusion.3), channel_id=1, source_target_pairs={{0,4},{4,0},{1,5},{5,1},{2,6},{6,2},{3,7},{7,3},{8,12},{12,8},{9,1... | collective-permute-start | bytes 104 | tf_op jit(solution)/shard_map/ppermute | solution.py:132
  6.1 3.6 %collective-permute-start.1 = (f32[8,1]{0,1:T(1,128)S(1)}, f32[8,1]{0,1:T(1,128)S(1)}, u32[]{:S(2)}, u32[]{:S(2)}) collective-permute-start(f32[8,1]{0,1:T(1,128)S(1)} %convolution_bitcast_fusion.2), channel_id=1, source_target_pairs={{0,4},{4,0},{1,5},{5,1},{2,6},{6,2},{3,7},{7,3},{8,12},{12,8},{9,1... | collective-permute-start | bytes 104 | tf_op jit(solution)/shard_map/ppermute | solution.py:132
  11.8 11.9 %all-to-all-start = ((bf16[96,1,4,2,128]{4,0,3,1,2:T(8,128)(2,1)}), bf16[96,1,4,2,128]{4,0,3,1,2:T(8,128)(2,1)S(1)}, u32[]{:S(2)}, u32[]{:S(2)}) async-start(bf16[96,1,4,2,128]{4,0,3,1,2:T(8,128)(2,1)} %fusion.94), calls=%async_computation | async-start | bytes 393216 | tf_op jit(solution)/shard_map/all_to_all | solution.py:161
  16.7 16.6 %slice-start = ((f32[1152]{0:T(1024)}), f32[384]{0:T(512)S(1)}, s32[]{:S(2)}) async-start(f32[1152]{0:T(1024)} %param.18), calls=%async_computation.3 | async-start | bytes 4096 | tf_op jit(solution)/shard_map/slice | solution.py:169
  18.6 39.7 %collective-permute-start.6 = (bf16[1,96,1,4,2,128]{5,4,3,1,2,0:T(2,128)(2,1)}, bf16[1,96,1,4,2,128]{5,4,3,1,2,0:T(2,128)(2,1)}, u32[]{:S(2)}, u32[]{:S(2)}) collective-permute-start(bf16[1,96,1,4,2,128]{5,4,3,1,2,0:T(2,128)(2,1)} %get-tuple-element.62), channel_id=1, source_target_pairs={{0,8},{8,0},{16,24},{24,16},{1,9},{9,1},{17,25},{25,17},{2,10},{10... | collective-permute-start | bytes 589832 | tf_op jit(solution)/shard_map/ppermute | solution.py:27
  20.7 37.7 %collective-permute-start.7 = (bf16[1,96,1,4,2,128]{5,4,3,1,2,0:T(2,128)(2,1)}, bf16[1,96,1,4,2,128]{5,4,3,1,2,0:T(2,128)(2,1)}, u32[]{:S(2)}, u32[]{:S(2)}) collective-permute-start(bf16[1,96,1,4,2,128]{5,4,3,1,2,0:T(2,128)(2,1)} %get-tuple-element.62), channel_id=1, source_target_pairs={{0,16},{8,24},{16,0},{24,8},{1,17},{9,25},{17,1},{25,9},{2,18},{10... | collective-permute-start | bytes 589832 | tf_op jit(solution)/shard_map/ppermute | solution.py:27
  23.0 35.3 %collective-permute-start.8 = (bf16[1,96,1,4,2,128]{5,4,3,1,2,0:T(2,128)(2,1)}, bf16[1,96,1,4,2,128]{5,4,3,1,2,0:T(2,128)(2,1)}, u32[]{:S(2)}, u32[]{:S(2)}) collective-permute-start(bf16[1,96,1,4,2,128]{5,4,3,1,2,0:T(2,128)(2,1)} %get-tuple-element.62), channel_id=1, source_target_pairs={{0,24},{8,16},{16,8},{24,0},{1,25},{9,17},{17,9},{25,1},{2,26},{10... | collective-permute-start | bytes 589832 | tf_op jit(solution)/shard_map/ppermute | solution.py:27
  24.3 9.9 %copy-start.9 = (f32[384]{0:T(512)S(1)}, f32[384]{0:T(512)}, u32[]{:S(2)}) copy-start(f32[384]{0:T(512)} %param.20) | copy-start | bytes 4612
  35.6 11.1 %all-to-all-start.1 = ((bf16[384,1,1,2,128]{4,3,2,1,0:T(2,128)(2,1)}), bf16[384,1,1,2,128]{4,3,2,1,0:T(2,128)(2,1)S(1)}, u32[]{:S(2)}, u32[]{:S(2)}) async-start(bf16[384,1,1,2,128]{4,3,2,1,0:T(2,128)(2,1)} %copy.32), calls=%async_computation.1 | async-start | bytes 393216 | tf_op jit(solution)/shard_map/all_to_all | solution.py:187
  40.5 6.3 %copy-start.3 = (bf16[96,1,4,2,128]{4,3,2,1,0:T(2,128)(2,1)S(1)}, bf16[96,1,4,2,128]{4,3,2,1,0:T(2,128)(2,1)}, u32[]{:S(2)}) copy-start(bf16[96,1,4,2,128]{4,3,2,1,0:T(2,128)(2,1)} %param.13) | copy-start | bytes 589828
  40.5 11.5 %copy-start.5 = (f32[96]{0:T(128)S(1)}, f32[96]{0:T(128)}, u32[]{:S(2)}) copy-start(f32[96]{0:T(128)} %param.22) | copy-start | bytes 1156
  40.5 11.5 %copy-start.6 = (f32[96]{0:T(128)S(1)}, f32[96]{0:T(128)}, u32[]{:S(2)}) copy-start(f32[96]{0:T(128)} %param.21) | copy-start | bytes 1156
  47.3 3.6 %collective-permute-start.2 = (f32[8,1]{0,1:T(1,128)S(1)}, f32[8,1]{0,1:T(1,128)S(1)}, u32[]{:S(2)}, u32[]{:S(2)}) collective-permute-start(f32[8,1]{0,1:T(1,128)S(1)} %convolution_bitcast_fusion.1), channel_id=1, source_target_pairs={{0,4},{4,0},{1,5},{5,1},{2,6},{6,2},{3,7},{7,3},{8,12},{12,8},{9,1... | collective-permute-start | bytes 104 | tf_op jit(solution)/shard_map/ppermute | solution.py:132
  48.1 3.6 %collective-permute-start.3 = (f32[8,1]{0,1:T(1,128)S(1)}, f32[8,1]{0,1:T(1,128)S(1)}, u32[]{:S(2)}, u32[]{:S(2)}) collective-permute-start(f32[8,1]{0,1:T(1,128)S(1)} %convolution_bitcast_fusion), channel_id=1, source_target_pairs={{0,4},{4,0},{1,5},{5,1},{2,6},{6,2},{3,7},{7,3},{8,12},{12,8},{9,1... | collective-permute-start | bytes 104 | tf_op jit(solution)/shard_map/ppermute | solution.py:132
  53.0 11.0 %collective-permute-start.4 = (bf16[96,1,4,1,128]{4,0,3,2,1:T(8,128)(2,1)}, bf16[96,1,4,1,128]{4,0,3,2,1:T(8,128)(2,1)}, u32[]{:S(2)}, u32[]{:S(2)}) collective-permute-start(bf16[96,1,4,1,128]{4,0,3,2,1:T(8,128)(2,1)} %get-tuple-element.63), channel_id=1, source_target_pairs={{0,4},{1,5},{2,6},{3,7},{8,12},{9,13},{10,14},{11,15},{16,20},{17,... | collective-permute-start | bytes 294920 | tf_op jit(solution)/shard_map/ppermute | solution.py:39
  57.1 7.0 %collective-permute-start.5 = (bf16[96,1,4,1,128]{4,0,3,2,1:T(8,128)(2,1)}, bf16[96,1,4,1,128]{4,0,3,2,1:T(8,128)(2,1)}, u32[]{:S(2)}, u32[]{:S(2)}) collective-permute-start(bf16[96,1,4,1,128]{4,0,3,2,1:T(8,128)(2,1)} %get-tuple-element.64), channel_id=1, source_target_pairs={{4,0},{5,1},{6,2},{7,3},{12,8},{13,9},{14,10},{15,11},{20,16},{21,... | collective-permute-start | bytes 294920 | tf_op jit(solution)/shard_map/ppermute | solution.py:40
  72.1 1.3 copy-start.4
  77.3 1.9 %copy-start.1 = (f32[2624,384]{1,0:T(8,128)}, f32[2624,384]{1,0:T(8,128)S(1)}, u32[]{:S(2)}) copy-start(f32[2624,384]{1,0:T(8,128)S(1)} %pad.10) | copy-start | bytes 12091396
  79.3 2.8 %collective-permute-start.9 = (bf16[1312,384]{1,0:T(8,128)(2,1)S(1)}, bf16[1312,384]{1,0:T(8,128)(2,1)}, u32[]{:S(2)}, u32[]{:S(2)}) collective-permute-start(bf16[1312,384]{1,0:T(8,128)(2,1)S(1)} %fusion.47), channel_id=1, source_target_pairs={{0,1},{1,0},{2,3},{3,2},{4,5},{5,4},{6,7},{7,6},{8,9},{9,8},{10,11... | collective-permute-start | bytes 3022856 | tf_op jit(solution)/shard_map/ppermute | solution.py:114
  85.0 13.8 %collective-permute-start.10 = (bf16[656,384]{1,0:T(8,128)(2,1)}, bf16[656,384]{1,0:T(8,128)(2,1)}, u32[]{:S(2)}, u32[]{:S(2)}) collective-permute-start(bf16[656,384]{1,0:T(8,128)(2,1)} %fusion.56), channel_id=1, source_target_pairs={{0,2},{1,3},{2,0},{3,1},{4,6},{5,7},{6,4},{7,5},{8,10},{9,11},{10,... | collective-permute-start | bytes 1511432 | tf_op jit(solution)/shard_map/ppermute | solution.py:114
  100.0 1.0 copy-start.2
  100.9 8.8 %collective-permute-start.11 = (bf16[328,384]{1,0:T(8,128)(2,1)S(1)}, bf16[328,384]{1,0:T(8,128)(2,1)S(1)}, u32[]{:S(2)}, u32[]{:S(2)}) collective-permute-start(bf16[328,384]{1,0:T(8,128)(2,1)S(1)} %fusion.89), channel_id=1, source_target_pairs={{0,4},{4,0},{1,5},{5,1},{2,6},{6,2},{3,7},{7,3},{8,12},{12,8},{9,1... | collective-permute-start | bytes 755720 | tf_op jit(solution)/shard_map/ppermute | solution.py:114
  110.9 6.8 %collective-permute-start.12 = (bf16[328,384]{1,0:T(8,128)(2,1)S(1)}, bf16[328,384]{1,0:T(8,128)(2,1)S(1)}, u32[]{:S(2)}, u32[]{:S(2)}) collective-permute-start(bf16[328,384]{1,0:T(8,128)(2,1)S(1)} %fusion.61), channel_id=1, source_target_pairs={{0,4},{4,0},{1,5},{5,1},{2,6},{6,2},{3,7},{7,3},{8,12},{12,8},{9,1... | collective-permute-start | bytes 755720 | tf_op jit(solution)/shard_map/ppermute | solution.py:120
  118.7 11.4 %collective-permute-start.13 = (bf16[656,384]{1,0:T(8,128)(2,1)}, bf16[656,384]{1,0:T(8,128)(2,1)S(1)}, u32[]{:S(2)}, u32[]{:S(2)}) collective-permute-start(bf16[656,384]{1,0:T(8,128)(2,1)} %get-tuple-element.57), channel_id=1, source_target_pairs={{0,2},{1,3},{2,0},{3,1},{4,6},{5,7},{6,4},{7,5},{8,10},{9,11},{10,... | collective-permute-start | bytes 1511432 | tf_op jit(solution)/shard_map/ppermute | solution.py:120
  121.6 21.6 %all-to-all-start.2 = ((bf16[4,96,1,4,2,128]{5,1,4,3,2,0:T(8,128)(2,1)}), bf16[4,96,1,4,2,128]{5,1,4,3,2,0:T(8,128)(2,1)S(1)}, u32[]{:S(2)}, u32[]{:S(2)}) async-start(bf16[4,96,1,4,2,128]{5,1,4,3,2,0:T(8,128)(2,1)} %copy.36), calls=%async_computation.2 | async-start | bytes 1572864 | tf_op jit(solution)/shard_map/all_to_all | solution.py:207
  130.6 12.7 %copy-start.7 = (f32[96]{0:T(128)S(1)}, f32[96]{0:T(128)}, u32[]{:S(2)}) copy-start(f32[96]{0:T(128)} %param.24) | copy-start | bytes 1156
  131.7 12.6 %collective-permute-start.14 = (bf16[1312,384]{1,0:T(8,128)(2,1)}, bf16[1312,384]{1,0:T(8,128)(2,1)S(1)}, u32[]{:S(2)}, u32[]{:S(2)}) collective-permute-start(bf16[1312,384]{1,0:T(8,128)(2,1)} %get-tuple-element.53), channel_id=1, source_target_pairs={{0,1},{1,0},{2,3},{3,2},{4,5},{5,4},{6,7},{7,6},{8,9},{9,8},{10,11... | collective-permute-start | bytes 3022856 | tf_op jit(solution)/shard_map/ppermute | solution.py:120
